TPU v7x, 128 devices: a whole 4x4x4 slice. The times are simulated.
128 devices in a mesh: gx: 16 (over y, z), gy: 8 (over x, core).
Axes of the slice: x: 4, y: 4, z: 4, core: 2. Of those that a mesh axis runs over, the one named last changes fastest.
Arguments:
- points: bfloat16 [1024, 128, 512], P(('gx', 'gy')), may hold values from -6 to 6
- moved_to: int32 [2, 2, 1024], P(None, None, ('gx', 'gy')), may hold values from 0 to 1023, as said below
- gains: float32 [2, 2, 512], replicated, may hold values from 0.1 to 1.9
- w_qkv: bfloat16 [2, 512, 1536], replicated, may hold values from -4 to 4
- w_out: bfloat16 [2, 512, 512], replicated, may hold values from -0.25 to 0.25
- w_up: bfloat16 [2, 512, 2048], replicated, may hold values from -0.25 to 0.25
- w_down: bfloat16 [2, 2048, 512], replicated, may hold values from -0.125 to 0.125
Outputs:
- encoded: bfloat16 [1024, 128, 512], P(('gx', 'gy'))
Inputs may be any that keep to these rules, and one draw needn't show every extreme that they name: Each moved_to[l, s] is a permutation of the 1024 positions. The owner of position p is p // 8, with owner index = gx index * 8 + gy index. Section 0 keeps every brick's gy index, section 1 its gx index. From one owner at most 2 bricks go to any one owner in section 0 and at most 2 in section 1; in every layer, section and group some owner sends exactly that many to one owner.
All inputs are finite; a program needn't handle non-finite values.
Results may differ from a plain program's by a relative error of at most 0.018.
Values may be sent and summed in bfloat16 or wider, within the bound.
A program may use at most 128 MiB of HBM per device.

v0:
```python
import functools
import math

import jax
import jax.numpy as jnp
from jax import lax
from jax.experimental import pallas as pl
from jax.experimental.pallas import tpu as pltpu
from jax.sharding import PartitionSpec as P

MESH = pl.DeviceIdType.MESH
F32 = jnp.float32
BF16 = jnp.bfloat16

LAYERS = 2
DEVICES = 128
GY = 8
D = 512
FF = 2048
FF_BLOCK = 512
HEAD_DIM = 16
PATCH = 512
GROUP = 128
HEADS = GROUP // HEAD_DIM
HALF = D // 2
ROWS = 2048
SCALE = math.log2(math.e) / math.sqrt(HEAD_DIM)


def iota(shape, dim):
    return lax.broadcasted_iota(jnp.int32, shape, dim)


def dot(a, b):
    return jnp.dot(a, b, preferred_element_type=F32)


def one_hot(hit):
    return jnp.where(hit, 1.0, 0.0).astype(BF16)


def row_norm(values, gain):
    center = values - jnp.mean(values, axis=1, keepdims=True)
    spread = jnp.mean(center * center, axis=1, keepdims=True)
    return center * lax.rsqrt(spread + 1e-05) * gain


def local_row(canonical):
    return (canonical % 4) * 128 + (canonical // 8) * 2 + (canonical // 4) % 2


def kernel(
    x_ref, moved_ref, gains_ref, qkv_hbm, out_hbm, up_hbm, down_hbm, o_ref,
    w_qkv, w_out, w_up, w_down, stage, mid, spread, final, table, order, qkv, probs, blocks, attended,
    weight_sem, local_sem, table_sems, send1, recv1, send2, recv2,
):
    me = lax.axis_index("gx") * GY + lax.axis_index("gy")

    def place(device):
        return (device // GY, device % GY)

    def each_peer(body):
        def step(i, carry):
            body((me + i) % DEVICES)
            return carry

        lax.fori_loop(1, DEVICES, step, 0)

    weights = []
    for i, (src, dst) in enumerate(
        ((qkv_hbm, w_qkv), (out_hbm, w_out), (up_hbm, w_up), (down_hbm, w_down))
    ):
        copy = pltpu.make_async_copy(src, dst, weight_sem.at[i])
        copy.start()
        weights.append(copy)

    barrier = pltpu.get_barrier_semaphore()
    each_peer(
        lambda p: pl.semaphore_signal(barrier, inc=1, device_id=place(p), device_id_type=MESH)
    )

    to_canonical = one_hot(
        iota((PATCH, PATCH), 1) == local_row(iota((PATCH, PATCH), 0))
    )
    for a in range(2):
        rows = dot(to_canonical, x_ref[a * PATCH : (a + 1) * PATCH, :])
        for h in range(2):
            stage[0, a, h] = rows[:, h * HALF : (h + 1) * HALF].reshape(64, 8, HALF).astype(BF16)
    table[me] = moved_ref[...]

    pl.semaphore_wait(barrier, DEVICES - 1)

    def send_table(p):
        pltpu.make_async_remote_copy(
            src_ref=moved_ref, dst_ref=table.at[me], send_sem=table_sems.at[0],
            recv_sem=table_sems.at[1], device_id=place(p), device_id_type=MESH,
        ).start()

    def send_spread(layer, a):
        def send(p):
            pltpu.make_async_remote_copy(
                src_ref=stage.at[layer, a, p % 2, p // 2], dst_ref=spread.at[layer, a, me],
                send_sem=send1.at[layer, a], recv_sem=recv1.at[layer, a],
                device_id=place(p), device_id_type=MESH,
            ).start()

        each_peer(send)
        own = pltpu.make_async_copy(
            stage.at[layer, a, me % 2, me // 2], spread.at[layer, a, me], local_sem
        )
        own.start()
        own.wait()

    def send_final(layer, a):
        def send(p):
            pltpu.make_async_remote_copy(
                src_ref=mid.at[layer, a, p], dst_ref=final.at[layer, a, me % 2, me // 2],
                send_sem=send2.at[layer, a], recv_sem=recv2.at[layer, a],
                device_id=place(p), device_id_type=MESH,
            ).start()

        each_peer(send)
        own = pltpu.make_async_copy(
            mid.at[layer, a, me], final.at[layer, a, me % 2, me // 2], local_sem
        )
        own.start()
        own.wait()

    def await_bytes(layer, a, sem):
        part = spread.at[layer, a, 0 : DEVICES - 1]
        pltpu.make_async_copy(part, part, sem.at[layer, a]).wait()

    each_peer(send_table)
    for a in range(2):
        send_spread(0, a)

    head_of = iota((PATCH, GROUP), 1) // HEAD_DIM
    for h in range(HEADS):
        blocks[h * PATCH : (h + 1) * PATCH, GROUP:] = one_hot(head_of == h)

    part = table.at[0 : DEVICES - 1]
    pltpu.make_async_copy(part, part, table_sems.at[1]).wait()
    pltpu.make_async_copy(part, part, table_sems.at[0]).wait()
    moves = table[...].reshape(DEVICES, DEVICES).astype(F32).T[0:32]
    high = jnp.floor(moves * (1 / 32))
    low = (moves - high * 32).astype(BF16)
    high = high.astype(BF16)

    def along(width, owner, slot):
        owners = one_hot(iota((DEVICES, width), 0) == owner(iota((DEVICES, width), 1)))
        hit = iota((32, width), 0) % 8 == slot(iota((32, width), 1))
        both = [jnp.where(hit, dot(v, owners), 0.0) for v in (high, low)]
        return lambda i: [
            jnp.sum(v[i * 8 : (i + 1) * 8], axis=0, keepdims=True) for v in both
        ]

    by_row = along(ROWS, lambda i: i // 8 % DEVICES, lambda i: i // 1024 * 4 + i % 4)
    by_brick = along(1024, lambda i: i // 8, lambda i: i % 8)
    for layer in range(LAYERS):
        first = by_row(2 * layer)
        first = first[0] * 32 + first[1]
        second = by_brick(2 * layer + 1)
        hit = one_hot(iota((1024, ROWS), 0).astype(F32) == first)
        both = jnp.concatenate(second, axis=0).astype(BF16)
        both = dot(jnp.concatenate([both] * 4, axis=0), hit)
        point = (iota((1, ROWS), 1) // 4 % 2).astype(F32)
        code = (both[0:1] * 32 + both[1:2]) * 2 + point
        for r in range(0, ROWS, 512):
            p = iota((512, 1), 0) + r
            want = (p // 8 % DEVICES * 8 + p // 1024 * 4 + p % 4) * 2 + p // 4 % 2
            order[layer, r : r + 512, :] = one_hot(want.astype(F32) == code)

    for copy in weights:
        copy.wait()

    def encode(layer, a):
        x = jnp.concatenate(
            [final[layer, a, h].astype(F32).reshape(PATCH, HALF) for h in range(2)], axis=1
        )
        normed = row_norm(x, gains_ref[layer, 0:1, :]).astype(BF16)
        qkv[:, 0:D] = (dot(normed, w_qkv[layer, :, 0:D]) * SCALE).astype(BF16)
        qkv[:, D:] = dot(normed, w_qkv[layer, :, D:]).astype(BF16)

        def group(g, carry):
            off = pl.multiple_of(g * GROUP, GROUP)
            query = qkv[:, pl.ds(off, GROUP)]
            keys = qkv[:, pl.ds(pl.multiple_of(D + off, GROUP), GROUP)]
            values = qkv[:, pl.ds(pl.multiple_of(2 * D + off, GROUP), GROUP)]
            zero = jnp.zeros((), BF16)
            for h in range(HEADS):
                rows = slice(h * PATCH, (h + 1) * PATCH)
                blocks[rows, 0:GROUP] = jnp.where(head_of == h, values, zero)
                scores = lax.dot_general(
                    jnp.where(head_of == h, query, zero), keys, (((1,), (1,)), ((), ())),
                    preferred_element_type=F32,
                )
                peak = jnp.max(scores, axis=1, keepdims=True)
                probs[:, rows] = jnp.exp2(scores - peak).astype(BF16)
            mixed = dot(probs[...], blocks[...])
            attended[:, pl.ds(off, GROUP)] = (mixed[:, 0:GROUP] / mixed[:, GROUP:]).astype(BF16)
            return carry

        lax.fori_loop(0, D // GROUP, group, 0)
        mixed = (x + dot(attended[...], w_out[layer])).astype(BF16).astype(F32)
        inner = row_norm(mixed, gains_ref[layer, 1:2, :]).astype(BF16)
        result = mixed
        for c in range(0, FF, FF_BLOCK):
            up = dot(inner, w_up[layer, :, c : c + FF_BLOCK])
            hidden = (0.5 * up * (1.0 + lax.erf(up * math.sqrt(0.5)))).astype(BF16)
            result = result + dot(hidden, w_down[layer, c : c + FF_BLOCK, :])
        return result

    def run_layer(layer, carry):
        for a in range(2):
            await_bytes(layer, a, recv1)
        rows = spread[layer].astype(F32).reshape(ROWS, HALF).astype(BF16)
        for a in range(2):
            half = dot(order[layer, a * 1024 : (a + 1) * 1024, :], rows)
            mid[layer, a] = half.reshape(DEVICES, 8, HALF).astype(BF16)
            send_final(layer, a)

        def patch(a, carry):
            await_bytes(layer, a, recv2)
            result = encode(layer, a)

            @pl.when(layer == 0)
            def _():
                for h in range(2):
                    columns = result[:, h * HALF : (h + 1) * HALF]
                    stage[1, a, h] = columns.reshape(64, 8, HALF).astype(BF16)
                send_spread(1, a)

            @pl.when(layer == LAYERS - 1)
            def _():
                to_local = one_hot(
                    iota((PATCH, PATCH), 0) == local_row(iota((PATCH, PATCH), 1))
                )
                rows = pl.ds(pl.multiple_of(a * PATCH, PATCH), PATCH)
                o_ref[rows, :] = dot(to_local, result.astype(BF16)).astype(BF16)

            return carry

        lax.fori_loop(0, 2, patch, 0)
        return carry

    lax.fori_loop(0, LAYERS, run_layer, 0)
    for layer in range(LAYERS):
        for a in range(2):
            await_bytes(layer, a, send1)
            await_bytes(layer, a, send2)


def per_device(points, moved_to, gains, w_qkv, w_out, w_up, w_down):
    x = points.reshape(2 * PATCH, D)
    moved = jnp.pad(moved_to.reshape(1, 32), ((0, 0), (0, DEVICES - 32)))
    vmem = pl.BlockSpec(memory_space=pltpu.VMEM)
    hbm = pl.BlockSpec(memory_space=pl.ANY)
    dma = pltpu.SemaphoreType.DMA
    out = pl.pallas_call(
        kernel,
        out_shape=jax.ShapeDtypeStruct(x.shape, BF16),
        in_specs=[vmem, vmem, vmem, hbm, hbm, hbm, hbm],
        out_specs=vmem,
        scratch_shapes=[
            pltpu.VMEM(w_qkv.shape, BF16),
            pltpu.VMEM(w_out.shape, BF16),
            pltpu.VMEM(w_up.shape, BF16),
            pltpu.VMEM(w_down.shape, BF16),
            pltpu.VMEM((LAYERS, 2, 2, 64, 8, HALF), BF16),
            pltpu.VMEM((LAYERS, 2, DEVICES, 8, HALF), BF16),
            pltpu.VMEM((LAYERS, 2, DEVICES, 8, HALF), BF16),
            pltpu.VMEM((LAYERS, 2, 2, 64, 8, HALF), BF16),
            pltpu.VMEM((DEVICES, 1, DEVICES), jnp.int32),
            pltpu.VMEM((LAYERS, ROWS, ROWS), BF16),
            pltpu.VMEM((PATCH, 3 * D), BF16),
            pltpu.VMEM((PATCH, HEADS * PATCH), BF16),
            pltpu.VMEM((HEADS * PATCH, 2 * GROUP), BF16),
            pltpu.VMEM((PATCH, D), BF16),
            dma((4,)),
            dma,
            dma((2,)),
            dma((LAYERS, 2)),
            dma((LAYERS, 2)),
            dma((LAYERS, 2)),
            dma((LAYERS, 2)),
        ],
        compiler_params=pltpu.CompilerParams(
            collective_id=0, has_side_effects=True, vmem_limit_bytes=63 * 2**20
        ),
    )(x, moved, gains, w_qkv, w_out, w_up, w_down)
    return out.reshape(points.shape)


def solution(mesh):
    placed = (P(("gx", "gy"), None, None), P(None, None, ("gx", "gy")), P(), P(), P(), P(), P())
    return jax.shard_map(
        per_device,
        mesh=mesh,
        in_specs=placed,
        out_specs=P(("gx", "gy"), None, None),
        check_vma=False,
    )
```

profile of v0, /device:TPU:9, one launch (start us, length us, event | category | flops | bytes accessed | tf_op | source)
XLA Modules:
  0.0 143.4 jit_solution(5458571646641246966)
XLA Ops:
  0.0 0.8 reshape.10
  0.8 0.5 pad.4.moved_ref
  1.3 139.8 %shard_map.73 = bf16[1024,512]{1,0:T(8,128)(2,1)} custom-call(bf16[1024,512]{1,0:T(8,128)(2,1)} %bitcast.3, s32[1,128]{1,0:T(1,128)} %pad.4.moved_ref, f32[2,2,512]{2,1,0:T(2,128)} %gains_ref.1, bf16[2,512,1536]{2,1,0:T(8,128)(2,1)} %qkv_hbm.1, bf16[2,512,512]{2,1,0:T(8,128)(2,1)} %out_hbm.1, bf16[2,512,2048]{2,1,0:T(8,128)(2,1)} %up_hbm.1, ...), custom_call_target="tpu_custom_call" | custom-call | tf_op jit(solution)/shard_map/pallas_call | solution.py:259
  141.1 2.3 %copy.9 = bf16[8,128,512]{2,1,0:T(8,128)(2,1)} copy(bf16[8,128,512]{2,1,0:T(8,128)(2,1)} %bitcast.2) | data formatting | bytes 2097152
where the time goes:
time: 144 us; the launch traced here: 143 us
  Pallas kernels  140 us (97%)
  local copies, waits for them, and re-layouts  3.54 us (2%)
    pallas_call x1, Pallas kernels, per_device(): pl.pallas_call(kernel, out_shape=jax.ShapeDtypeStruct(x.shape, BF16), in_...  140 us

commit v1 on v0

--- a/solution.py
+++ b/solution.py
@@ -25,6 +25,20 @@
 HALF = D // 2
 ROWS = 2048
 SCALE = math.log2(math.e) / math.sqrt(HEAD_DIM)
+NT = (((1,), (1,)), ((), ()))
+TN = (((0,), (0,)), ((), ()))
+TILE = 128
+STEP = (0, 1, 3, 2)
+
+
+def farthest_first():
+    found = [
+        (bin(v).count("1"), (v * 37 + c) % 64, (STEP[v >> 4], STEP[v >> 2 & 3], STEP[v & 3], c))
+        for v in range(64)
+        for c in range(2)
+        if v or c
+    ]
+    return [offset for _, _, offset in sorted(found, key=lambda f: (-f[0], f[1]))]
 
 
 def iota(shape, dim):
@@ -51,20 +65,21 @@
 
 def kernel(
     x_ref, moved_ref, gains_ref, qkv_hbm, out_hbm, up_hbm, down_hbm, o_ref,
-    w_qkv, w_out, w_up, w_down, stage, mid, spread, final, table, order, qkv, probs, blocks, attended,
+    w_qkv, w_out, w_up, w_down, stage, mid, spread, final, table, moved, order,
+    w_values, qk, values, probs, attended,
     weight_sem, local_sem, table_sems, send1, recv1, send2, recv2,
 ):
-    me = lax.axis_index("gx") * GY + lax.axis_index("gy")
-
-    def place(device):
-        return (device // GY, device % GY)
+    row, column = lax.axis_index("gx"), lax.axis_index("gy")
+    me = row * GY + column
+    ys = [(row // 4 + i) % 4 * 4 for i in range(4)]
+    zs = [(row + i) % 4 for i in range(4)]
+    xs = [(column // 2 + i) % 4 * 2 for i in range(4)]
+    cores = [(column + i) % 2 for i in range(2)]
 
     def each_peer(body):
-        def step(i, carry):
-            body((me + i) % DEVICES)
-            return carry
-
-        lax.fori_loop(1, DEVICES, step, 0)
+        for y, z, x, c in farthest_first():
+            there = (ys[y] + zs[z], xs[x] + cores[c])
+            body(there[0] * GY + there[1], there)
 
     weights = []
     for i, (src, dst) in enumerate(
@@ -76,7 +91,7 @@
 
     barrier = pltpu.get_barrier_semaphore()
     each_peer(
-        lambda p: pl.semaphore_signal(barrier, inc=1, device_id=place(p), device_id_type=MESH)
+        lambda p, at: pl.semaphore_signal(barrier, inc=1, device_id=at, device_id_type=MESH)
     )
 
     to_canonical = one_hot(
@@ -86,37 +101,41 @@
         rows = dot(to_canonical, x_ref[a * PATCH : (a + 1) * PATCH, :])
         for h in range(2):
             stage[0, a, h] = rows[:, h * HALF : (h + 1) * HALF].reshape(64, 8, HALF).astype(BF16)
-    table[me] = moved_ref[...]
+    parts = [moved_ref[l, s : s + 1, :] for l in range(LAYERS) for s in range(2)]
+    moved[...] = jnp.concatenate(parts + [jnp.zeros((1, DEVICES - 32), jnp.int32)], axis=1)
+    table[me] = moved[...]
 
     pl.semaphore_wait(barrier, DEVICES - 1)
 
-    def send_table(p):
+    def send_table(p, at):
         pltpu.make_async_remote_copy(
-            src_ref=moved_ref, dst_ref=table.at[me], send_sem=table_sems.at[0],
-            recv_sem=table_sems.at[1], device_id=place(p), device_id_type=MESH,
+            src_ref=moved, dst_ref=table.at[me], send_sem=table_sems.at[0],
+            recv_sem=table_sems.at[1], device_id=at, device_id_type=MESH,
         ).start()
 
-    def send_spread(layer, a):
-        def send(p):
-            pltpu.make_async_remote_copy(
-                src_ref=stage.at[layer, a, p % 2, p // 2], dst_ref=spread.at[layer, a, me],
-                send_sem=send1.at[layer, a], recv_sem=recv1.at[layer, a],
-                device_id=place(p), device_id_type=MESH,
-            ).start()
+    def send_spread(layer, parts):
+        def send(p, at):
+            for a in parts:
+                pltpu.make_async_remote_copy(
+                    src_ref=stage.at[layer, a, p % 2, p // 2], dst_ref=spread.at[layer, a, me],
+                    send_sem=send1.at[layer, a], recv_sem=recv1.at[layer, a],
+                    device_id=at, device_id_type=MESH,
+                ).start()
 
         each_peer(send)
-        own = pltpu.make_async_copy(
-            stage.at[layer, a, me % 2, me // 2], spread.at[layer, a, me], local_sem
-        )
-        own.start()
-        own.wait()
+        for a in parts:
+            own = pltpu.make_async_copy(
+                stage.at[layer, a, me % 2, me // 2], spread.at[layer, a, me], local_sem
+            )
+            own.start()
+            own.wait()
 
     def send_final(layer, a):
-        def send(p):
+        def send(p, at):
             pltpu.make_async_remote_copy(
                 src_ref=mid.at[layer, a, p], dst_ref=final.at[layer, a, me % 2, me // 2],
                 send_sem=send2.at[layer, a], recv_sem=recv2.at[layer, a],
-                device_id=place(p), device_id_type=MESH,
+                device_id=at, device_id_type=MESH,
             ).start()
 
         each_peer(send)
@@ -131,12 +150,7 @@
         pltpu.make_async_copy(part, part, sem.at[layer, a]).wait()
 
     each_peer(send_table)
-    for a in range(2):
-        send_spread(0, a)
-
-    head_of = iota((PATCH, GROUP), 1) // HEAD_DIM
-    for h in range(HEADS):
-        blocks[h * PATCH : (h + 1) * PATCH, GROUP:] = one_hot(head_of == h)
+    send_spread(0, range(2))
 
     part = table.at[0 : DEVICES - 1]
     pltpu.make_async_copy(part, part, table_sems.at[1]).wait()
@@ -172,36 +186,58 @@
 
     for copy in weights:
         copy.wait()
+    for layer in range(LAYERS):
+        w_values[layer] = w_qkv[layer, :, 2 * D :].astype(F32).T.astype(BF16)
+    values[:, HEAD_DIM:, :] = jnp.ones((D // HEAD_DIM, HEAD_DIM, PATCH), BF16)
+    head_of = iota((PATCH, GROUP), 1) // HEAD_DIM
 
     def encode(layer, a):
         x = jnp.concatenate(
             [final[layer, a, h].astype(F32).reshape(PATCH, HALF) for h in range(2)], axis=1
         )
         normed = row_norm(x, gains_ref[layer, 0:1, :]).astype(BF16)
-        qkv[:, 0:D] = (dot(normed, w_qkv[layer, :, 0:D]) * SCALE).astype(BF16)
-        qkv[:, D:] = dot(normed, w_qkv[layer, :, D:]).astype(BF16)
+        qk[:, 0:D] = (dot(normed, w_qkv[layer, :, 0:D]) * SCALE).astype(BF16)
+        qk[:, D:] = dot(normed, w_qkv[layer, :, D : 2 * D]).astype(BF16)
+        turned = lax.dot_general(w_values[layer], normed, NT, preferred_element_type=F32)
+        values[:, 0:HEAD_DIM, :] = turned.reshape(D // HEAD_DIM, HEAD_DIM, PATCH).astype(BF16)
 
         def group(g, carry):
             off = pl.multiple_of(g * GROUP, GROUP)
-            query = qkv[:, pl.ds(off, GROUP)]
-            keys = qkv[:, pl.ds(pl.multiple_of(D + off, GROUP), GROUP)]
-            values = qkv[:, pl.ds(pl.multiple_of(2 * D + off, GROUP), GROUP)]
+            query = qk[:, pl.ds(off, GROUP)]
+            keys = qk[:, pl.ds(pl.multiple_of(D + off, GROUP), GROUP)]
             zero = jnp.zeros((), BF16)
-            for h in range(HEADS):
-                rows = slice(h * PATCH, (h + 1) * PATCH)
-                blocks[rows, 0:GROUP] = jnp.where(head_of == h, values, zero)
-                scores = lax.dot_general(
-                    jnp.where(head_of == h, query, zero), keys, (((1,), (1,)), ((), ())),
-                    preferred_element_type=F32,
-                )
-                peak = jnp.max(scores, axis=1, keepdims=True)
-                probs[:, rows] = jnp.exp2(scores - peak).astype(BF16)
-            mixed = dot(probs[...], blocks[...])
-            attended[:, pl.ds(off, GROUP)] = (mixed[:, 0:GROUP] / mixed[:, GROUP:]).astype(BF16)
+
+            def mix(h):
+                out = dot(values[g * HEADS + h], probs[h])
+                rows = pl.ds(pl.multiple_of((g * HEADS + h) * HEAD_DIM, HEAD_DIM), HEAD_DIM)
+                attended[rows, :] = (out[0:HEAD_DIM] / out[HEAD_DIM : HEAD_DIM + 1]).astype(BF16)
+
+            for h in range(0, HEADS + 2, 2):
+                scores = []
+                if h < HEADS:
+                    masked = jnp.concatenate(
+                        [jnp.where(head_of == h + i, keys, zero) for i in range(2)], axis=0
+                    )
+                    scores = [
+                        lax.dot_general(
+                            masked, query[c : c + TILE], NT, preferred_element_type=F32
+                        )
+                        for c in range(0, PATCH, TILE)
+                    ]
+                if h >= 2:
+                    mix(h - 2)
+                    mix(h - 1)
+                for i in range(2):
+                    for c, tile in enumerate(scores):
+                        tile = tile[i * PATCH : (i + 1) * PATCH]
+                        peak = jnp.max(tile, axis=0, keepdims=True)
+                        columns = slice(c * TILE, (c + 1) * TILE)
+                        probs[h + i, :, columns] = jnp.exp2(tile - peak).astype(BF16)
             return carry
 
         lax.fori_loop(0, D // GROUP, group, 0)
-        mixed = (x + dot(attended[...], w_out[layer])).astype(BF16).astype(F32)
+        projected = lax.dot_general(attended[...], w_out[layer], TN, preferred_element_type=F32)
+        mixed = (x + projected).astype(BF16).astype(F32)
         inner = row_norm(mixed, gains_ref[layer, 1:2, :]).astype(BF16)
         result = mixed
         for c in range(0, FF, FF_BLOCK):
@@ -228,7 +264,7 @@
                 for h in range(2):
                     columns = result[:, h * HALF : (h + 1) * HALF]
                     stage[1, a, h] = columns.reshape(64, 8, HALF).astype(BF16)
-                send_spread(1, a)
+                send_spread(1, (a,))
 
             @pl.when(layer == LAYERS - 1)
             def _():
@@ -252,7 +288,6 @@
 
 def per_device(points, moved_to, gains, w_qkv, w_out, w_up, w_down):
     x = points.reshape(2 * PATCH, D)
-    moved = jnp.pad(moved_to.reshape(1, 32), ((0, 0), (0, DEVICES - 32)))
     vmem = pl.BlockSpec(memory_space=pltpu.VMEM)
     hbm = pl.BlockSpec(memory_space=pl.ANY)
     dma = pltpu.SemaphoreType.DMA
@@ -271,11 +306,13 @@
             pltpu.VMEM((LAYERS, 2, DEVICES, 8, HALF), BF16),
             pltpu.VMEM((LAYERS, 2, 2, 64, 8, HALF), BF16),
             pltpu.VMEM((DEVICES, 1, DEVICES), jnp.int32),
+            pltpu.VMEM((1, DEVICES), jnp.int32),
             pltpu.VMEM((LAYERS, ROWS, ROWS), BF16),
-            pltpu.VMEM((PATCH, 3 * D), BF16),
-            pltpu.VMEM((PATCH, HEADS * PATCH), BF16),
-            pltpu.VMEM((HEADS * PATCH, 2 * GROUP), BF16),
-            pltpu.VMEM((PATCH, D), BF16),
+            pltpu.VMEM((LAYERS, D, D), BF16),
+            pltpu.VMEM((PATCH, 2 * D), BF16),
+            pltpu.VMEM((D // HEAD_DIM, 2 * HEAD_DIM, PATCH), BF16),
+            pltpu.VMEM((HEADS, PATCH, PATCH), BF16),
+            pltpu.VMEM((D, PATCH), BF16),
             dma((4,)),
             dma,
             dma((2,)),
@@ -287,7 +324,7 @@
         compiler_params=pltpu.CompilerParams(
             collective_id=0, has_side_effects=True, vmem_limit_bytes=63 * 2**20
         ),
-    )(x, moved, gains, w_qkv, w_out, w_up, w_down)
+    )(x, moved_to, gains, w_qkv, w_out, w_up, w_down)
     return out.reshape(points.shape)
 
 

time: 144 us -> 125 us (0.87)
  the two profiles are of different devices: /device:TPU:9 before, /device:TPU:1 now
where the time goes in v1:
time: 125 us; the launch traced here: 123 us
  Pallas kernels  120 us (96%)
  local copies, waits for them, and re-layouts  2.26 us (2%)
    pallas_call x1, Pallas kernels, per_device(): pl.pallas_call(kernel, out_shape=jax.ShapeDtypeStruct(x.shape, BF16), in_...  120 us

profile of v1, /device:TPU:1, one launch (start us, length us, event | category | flops | bytes accessed | tf_op | source)
XLA Modules:
  0.0 122.6 jit_solution(8464908358760309851)
XLA Ops:
  0.0 120.3 %shard_map.73 = bf16[1024,512]{1,0:T(8,128)(2,1)} custom-call(bf16[1024,512]{1,0:T(8,128)(2,1)} %bitcast.3, s32[2,2,8]{2,1,0:T(2,128)} %moved_ref.1, f32[2,2,512]{2,1,0:T(2,128)} %gains_ref.1, bf16[2,512,1536]{2,1,0:T(8,128)(2,1)} %qkv_hbm.1, bf16[2,512,512]{2,1,0:T(8,128)(2,1)} %out_hbm.1, bf16[2,512,2048]{2,1,0:T(8,128)(2,1)} %up_hbm.1, ...), custom_call_target="tpu_custom_call" | custom-call | tf_op jit(solution)/shard_map/pallas_call | solution.py:294
  120.3 2.3 %copy.9 = bf16[8,128,512]{2,1,0:T(8,128)(2,1)} copy(bf16[8,128,512]{2,1,0:T(8,128)(2,1)} %bitcast.2) | data formatting | bytes 2097152

commit v2 on v1

--- a/solution.py
+++ b/solution.py
@@ -170,7 +170,8 @@
 
     by_row = along(ROWS, lambda i: i // 8 % DEVICES, lambda i: i // 1024 * 4 + i % 4)
     by_brick = along(1024, lambda i: i // 8, lambda i: i % 8)
-    for layer in range(LAYERS):
+
+    def build_order(layer):
         first = by_row(2 * layer)
         first = first[0] * 32 + first[1]
         second = by_brick(2 * layer + 1)
@@ -184,10 +185,13 @@
             want = (p // 8 % DEVICES * 8 + p // 1024 * 4 + p % 4) * 2 + p // 4 % 2
             order[layer, r : r + 512, :] = one_hot(want.astype(F32) == code)
 
+    def turn_weights(layer):
+        w_values[layer] = w_qkv[layer, :, 2 * D :].astype(F32).T.astype(BF16)
+
     for copy in weights:
         copy.wait()
-    for layer in range(LAYERS):
-        w_values[layer] = w_qkv[layer, :, 2 * D :].astype(F32).T.astype(BF16)
+    build_order(0)
+    turn_weights(0)
     values[:, HEAD_DIM:, :] = jnp.ones((D // HEAD_DIM, HEAD_DIM, PATCH), BF16)
     head_of = iota((PATCH, GROUP), 1) // HEAD_DIM
 
@@ -212,27 +216,23 @@
                 rows = pl.ds(pl.multiple_of((g * HEADS + h) * HEAD_DIM, HEAD_DIM), HEAD_DIM)
                 attended[rows, :] = (out[0:HEAD_DIM] / out[HEAD_DIM : HEAD_DIM + 1]).astype(BF16)
 
-            for h in range(0, HEADS + 2, 2):
+            for h in range(HEADS + 1):
                 scores = []
                 if h < HEADS:
-                    masked = jnp.concatenate(
-                        [jnp.where(head_of == h + i, keys, zero) for i in range(2)], axis=0
-                    )
+                    masked = jnp.where(head_of == h, keys, zero)
                     scores = [
                         lax.dot_general(
                             masked, query[c : c + TILE], NT, preferred_element_type=F32
                         )
                         for c in range(0, PATCH, TILE)
                     ]
-                if h >= 2:
-                    mix(h - 2)
+                if h >= 1:
                     mix(h - 1)
-                for i in range(2):
-                    for c, tile in enumerate(scores):
-                        tile = tile[i * PATCH : (i + 1) * PATCH]
-                        peak = jnp.max(tile, axis=0, keepdims=True)
-                        columns = slice(c * TILE, (c + 1) * TILE)
-                        probs[h + i, :, columns] = jnp.exp2(tile - peak).astype(BF16)
+                for c in range(0, len(scores), 2):
+                    pair = jnp.concatenate(scores[c : c + 2], axis=1)
+                    peak = jnp.max(pair, axis=0, keepdims=True)
+                    columns = slice(c * TILE, (c + 2) * TILE)
+                    probs[h, :, columns] = jnp.exp2(pair - peak).astype(BF16)
             return carry
 
         lax.fori_loop(0, D // GROUP, group, 0)
@@ -247,13 +247,25 @@
         return result
 
     def run_layer(layer, carry):
+        halves = []
         for a in range(2):
             await_bytes(layer, a, recv1)
-        rows = spread[layer].astype(F32).reshape(ROWS, HALF).astype(BF16)
-        for a in range(2):
-            half = dot(order[layer, a * 1024 : (a + 1) * 1024, :], rows)
-            mid[layer, a] = half.reshape(DEVICES, 8, HALF).astype(BF16)
-            send_final(layer, a)
+            rows = spread[layer, a].astype(F32).reshape(1024, HALF).astype(BF16)
+            if a == 0:
+                halves = [
+                    dot(order[layer, b * 1024 : (b + 1) * 1024, 0:1024], rows) for b in range(2)
+                ]
+        for b in range(2):
+            half = halves[b] + dot(order[layer, b * 1024 : (b + 1) * 1024, 1024:], rows)
+            mid[layer, b] = half.reshape(DEVICES, 8, HALF).astype(BF16)
+            if b == 1:
+                await_bytes(layer, 0, send2)
+            send_final(layer, b)
+
+        @pl.when(layer == 0)
+        def _():
+            build_order(1)
+            turn_weights(1)
 
         def patch(a, carry):
             await_bytes(layer, a, recv2)
@@ -268,11 +280,7 @@
 
             @pl.when(layer == LAYERS - 1)
             def _():
-                to_local = one_hot(
-                    iota((PATCH, PATCH), 0) == local_row(iota((PATCH, PATCH), 1))
-                )
-                rows = pl.ds(pl.multiple_of(a * PATCH, PATCH), PATCH)
-                o_ref[rows, :] = dot(to_local, result.astype(BF16)).astype(BF16)
+                o_ref[pl.ds(pl.multiple_of(a * PATCH, PATCH), PATCH), :] = result.astype(BF16)
 
             return carry
 
@@ -283,7 +291,12 @@
     for layer in range(LAYERS):
         for a in range(2):
             await_bytes(layer, a, send1)
-            await_bytes(layer, a, send2)
+        await_bytes(layer, 1, send2)
+
+
+def to_local_order(x_ref, o_ref):
+    hit = iota((PATCH, PATCH), 0) == local_row(iota((PATCH, PATCH), 1))
+    o_ref[...] = dot(one_hot(hit), x_ref[...]).astype(BF16)
 
 
 def per_device(points, moved_to, gains, w_qkv, w_out, w_up, w_down):
@@ -325,6 +338,14 @@
             collective_id=0, has_side_effects=True, vmem_limit_bytes=63 * 2**20
         ),
     )(x, moved_to, gains, w_qkv, w_out, w_up, w_down)
+    half = pl.BlockSpec((PATCH, D), lambda a: (a, 0))
+    out = pl.pallas_call(
+        to_local_order,
+        grid=(2,),
+        in_specs=[half],
+        out_specs=half,
+        out_shape=jax.ShapeDtypeStruct(x.shape, BF16),
+    )(out)
     return out.reshape(points.shape)
 
 

time: 125 us -> 120 us (0.960); the launches traced: 123 us -> 120 us
  local copies, waits for them, and re-layouts: 2.26 us -> 0 us
    pallas_call x1, Pallas kernels: 120 us -> 117 us  [per_device(): pl.pallas_call(kernel, out_shape=jax.ShapeDtypeStruct(x.shape, BF16), in_...]
    pallas_call x0 -> x1, Pallas kernels: none -> 2.73 us  [per_device(): pl.pallas_call(to_local_order, grid=(2,), in_specs=[half], out_specs=half...]
    unnamed x1 -> x0, local copies, waits for them, and re-layouts: 2.26 us -> none
where the time goes in v2:
time: 120 us
  Pallas kernels  120 us (100%)
    pallas_call x1, Pallas kernels, per_device(): pl.pallas_call(kernel, out_shape=jax.ShapeDtypeStruct(x.shape, BF16), in_...  117 us
    pallas_call x1, Pallas kernels, per_device(): pl.pallas_call(to_local_order, grid=(2,), in_specs=[half], out_specs=half...  2.73 us

profile of v2, /device:TPU:1, one launch (start us, length us, event | category | flops | bytes accessed | tf_op | source)
XLA Modules:
  0.0 119.6 jit_solution(1150197407133090941)
XLA Ops:
  0.0 116.8 %shard_map.73.x_ref = bf16[1024,512]{1,0:T(8,128)(2,1)} custom-call(bf16[1024,512]{1,0:T(8,128)(2,1)} %bitcast.2, s32[2,2,8]{2,1,0:T(2,128)} %moved_ref.1, f32[2,2,512]{2,1,0:T(2,128)} %gains_ref.1, bf16[2,512,1536]{2,1,0:T(8,128)(2,1)} %qkv_hbm.1, bf16[2,512,512]{2,1,0:T(8,128)(2,1)} %out_hbm.1, bf16[2,512,2048]{2,1,0:T(8,128)(2,1)} %up_hbm.1, ...), custom_call_target="tpu_custom_call" | custom-call | tf_op jit(solution)/shard_map/pallas_call | solution.py:307
  116.9 2.7 %shard_map.74 = bf16[1024,512]{1,0:T(8,128)(2,1)} custom-call(bf16[1024,512]{1,0:T(8,128)(2,1)} %shard_map.73.x_ref), custom_call_target="tpu_custom_call" | custom-call | tf_op jit(solution)/shard_map/pallas_call | solution.py:342

commit v3 on v2

--- a/solution.py
+++ b/solution.py
@@ -28,6 +28,7 @@
 NT = (((1,), (1,)), ((), ()))
 TN = (((0,), (0,)), ((), ()))
 TILE = 128
+JOINED = 4
 STEP = (0, 1, 3, 2)
 
 
@@ -206,20 +207,21 @@
         values[:, 0:HEAD_DIM, :] = turned.reshape(D // HEAD_DIM, HEAD_DIM, PATCH).astype(BF16)
 
         def group(g, carry):
-            off = pl.multiple_of(g * GROUP, GROUP)
-            query = qk[:, pl.ds(off, GROUP)]
-            keys = qk[:, pl.ds(pl.multiple_of(D + off, GROUP), GROUP)]
             zero = jnp.zeros((), BF16)
 
             def mix(h):
-                out = dot(values[g * HEADS + h], probs[h])
-                rows = pl.ds(pl.multiple_of((g * HEADS + h) * HEAD_DIM, HEAD_DIM), HEAD_DIM)
+                head = g * (JOINED * HEADS) + h
+                out = dot(values[head], probs[h % HEADS])
+                rows = pl.ds(pl.multiple_of(head * HEAD_DIM, HEAD_DIM), HEAD_DIM)
                 attended[rows, :] = (out[0:HEAD_DIM] / out[HEAD_DIM : HEAD_DIM + 1]).astype(BF16)
 
-            for h in range(HEADS + 1):
+            for h in range(JOINED * HEADS + 1):
                 scores = []
-                if h < HEADS:
-                    masked = jnp.where(head_of == h, keys, zero)
+                if h < JOINED * HEADS:
+                    off = pl.multiple_of((g * JOINED + h // HEADS) * GROUP, GROUP)
+                    query = qk[:, pl.ds(off, GROUP)]
+                    keys = qk[:, pl.ds(pl.multiple_of(D + off, GROUP), GROUP)]
+                    masked = jnp.where(head_of == h % HEADS, keys, zero)
                     scores = [
                         lax.dot_general(
                             masked, query[c : c + TILE], NT, preferred_element_type=F32
@@ -232,10 +234,10 @@
                     pair = jnp.concatenate(scores[c : c + 2], axis=1)
                     peak = jnp.max(pair, axis=0, keepdims=True)
                     columns = slice(c * TILE, (c + 2) * TILE)
-                    probs[h, :, columns] = jnp.exp2(pair - peak).astype(BF16)
+                    probs[h % HEADS, :, columns] = jnp.exp2(pair - peak).astype(BF16)
             return carry
 
-        lax.fori_loop(0, D // GROUP, group, 0)
+        lax.fori_loop(0, D // GROUP // JOINED, group, 0)
         projected = lax.dot_general(attended[...], w_out[layer], TN, preferred_element_type=F32)
         mixed = (x + projected).astype(BF16).astype(F32)
         inner = row_norm(mixed, gains_ref[layer, 1:2, :]).astype(BF16)

time: 120 us -> 115 us (0.958)
  Pallas kernels: 120 us -> 115 us
    pallas_call x1, Pallas kernels: 117 us -> 112 us  [per_device(): pl.pallas_call(kernel, out_shape=jax.ShapeDtypeStruct(x.shape, BF16), in_...]
where the time goes in v3:
time: 115 us
  Pallas kernels  115 us (100%)
    pallas_call x1, Pallas kernels, per_device(): pl.pallas_call(kernel, out_shape=jax.ShapeDtypeStruct(x.shape, BF16), in_...  112 us
    pallas_call x1, Pallas kernels, per_device(): pl.pallas_call(to_local_order, grid=(2,), in_specs=[half], out_specs=half...  2.74 us

profile of v3, /device:TPU:1, one launch (start us, length us, event | category | flops | bytes accessed | tf_op | source)
XLA Modules:
  0.0 114.9 jit_solution(6655661315379955145)
XLA Ops:
  0.0 112.2 %shard_map.73.x_ref = bf16[1024,512]{1,0:T(8,128)(2,1)} custom-call(bf16[1024,512]{1,0:T(8,128)(2,1)} %bitcast.2, s32[2,2,8]{2,1,0:T(2,128)} %moved_ref.1, f32[2,2,512]{2,1,0:T(2,128)} %gains_ref.1, bf16[2,512,1536]{2,1,0:T(8,128)(2,1)} %qkv_hbm.1, bf16[2,512,512]{2,1,0:T(8,128)(2,1)} %out_hbm.1, bf16[2,512,2048]{2,1,0:T(8,128)(2,1)} %up_hbm.1, ...), custom_call_target="tpu_custom_call" | custom-call | tf_op jit(solution)/shard_map/pallas_call | solution.py:309
  112.2 2.7 %shard_map.74 = bf16[1024,512]{1,0:T(8,128)(2,1)} custom-call(bf16[1024,512]{1,0:T(8,128)(2,1)} %shard_map.73.x_ref), custom_call_target="tpu_custom_call" | custom-call | tf_op jit(solution)/shard_map/pallas_call | solution.py:344

commit v4 on v3

--- a/solution.py
+++ b/solution.py
@@ -260,17 +260,23 @@
         for b in range(2):
             half = halves[b] + dot(order[layer, b * 1024 : (b + 1) * 1024, 1024:], rows)
             mid[layer, b] = half.reshape(DEVICES, 8, HALF).astype(BF16)
-            if b == 1:
-                await_bytes(layer, 0, send2)
-            send_final(layer, b)
+            if b == 0:
+                send_final(layer, 0)
 
         @pl.when(layer == 0)
         def _():
             build_order(1)
             turn_weights(1)
 
+        await_bytes(layer, 0, send2)
+        await_bytes(layer, 0, recv2)
+        send_final(layer, 1)
+
         def patch(a, carry):
-            await_bytes(layer, a, recv2)
+            @pl.when(a == 1)
+            def _():
+                await_bytes(layer, 1, recv2)
+
             result = encode(layer, a)
 
             @pl.when(layer == 0)

time: 115 us -> 116 us (level)
  no operation moved by 1% of the time
where the time goes in v4:
time: 116 us
  Pallas kernels  116 us (100%)
    pallas_call x1, Pallas kernels, per_device(): pl.pallas_call(kernel, out_shape=jax.ShapeDtypeStruct(x.shape, BF16), in_...  113 us
    pallas_call x1, Pallas kernels, per_device(): pl.pallas_call(to_local_order, grid=(2,), in_specs=[half], out_specs=half...  2.74 us

profile of v4, /device:TPU:1, one launch (start us, length us, event | category | flops | bytes accessed | tf_op | source)
XLA Modules:
  0.0 116.1 jit_solution(11071532849135258827)
XLA Ops:
  0.0 113.3 %shard_map.73.x_ref = bf16[1024,512]{1,0:T(8,128)(2,1)} custom-call(bf16[1024,512]{1,0:T(8,128)(2,1)} %bitcast.2, s32[2,2,8]{2,1,0:T(2,128)} %moved_ref.1, f32[2,2,512]{2,1,0:T(2,128)} %gains_ref.1, bf16[2,512,1536]{2,1,0:T(8,128)(2,1)} %qkv_hbm.1, bf16[2,512,512]{2,1,0:T(8,128)(2,1)} %out_hbm.1, bf16[2,512,2048]{2,1,0:T(8,128)(2,1)} %up_hbm.1, ...), custom_call_target="tpu_custom_call" | custom-call | tf_op jit(solution)/shard_map/pallas_call | solution.py:315
  113.3 2.7 %shard_map.74 = bf16[1024,512]{1,0:T(8,128)(2,1)} custom-call(bf16[1024,512]{1,0:T(8,128)(2,1)} %shard_map.73.x_ref), custom_call_target="tpu_custom_call" | custom-call | tf_op jit(solution)/shard_map/pallas_call | solution.py:350
